TPU v7x, 32 devices: a whole 2x2x4 slice. The times are simulated.
32 devices in a mesh: freq: 4 (over y, core), stcol: 8 (over z, x).
Axes of the slice: x: 2, y: 2, z: 4, core: 2. Of those that a mesh axis runs over, the one named last changes fastest.
Arguments:
- visibilities: float32 [2, 4, 512, 1, 512], P(None, 'freq', 'stcol'), may hold values from -28.8 to 28.8
- positions: float32 [3, 1, 512], replicated, may hold values from -3 to 3
- source_lmn: float32 [3, 1024], replicated, may hold values from -0.5 to 0.5
- source_flux: float32 [1024], replicated, may hold values from 0.02 to 0.2
- cluster_map: int32 [1024], replicated, may hold values from 0 to 15, as said below
- station_order: int32 [512], replicated, may hold values from 0 to 511, each once
- penalty: float32 [16], replicated, may hold values from 9.8304 to 196.608
- offsets: float32 [2, 4, 16, 512], P(None, 'freq'), may hold values from -1.2 to 1.2
Outputs:
- gains: float32 [2, 4, 16, 512], P(None, 'freq', None, 'stcol')
- consensus: float32 [2, 4, 16, 512], P(None, 'freq', None, 'stcol')
Inputs may be any that keep to these rules, and one draw needn't show every extreme that they name: `cluster_map`: each of the 16 directions is named by exactly 64 sources. `station_order`: every station stands exactly once.
All inputs are finite; a program needn't handle non-finite values.
Results may differ from a plain program's by a relative error of at most 0.00011.
Values sent between devices are 32-bit elements; how exact they have to be, the bound alone decides.
A program may use at most 64 MiB of HBM per device.

v0:
```python
import math
import jax
import jax.numpy as jnp
from jax import lax
from jax.sharding import PartitionSpec as P

ADMM = 2
PASSES = 2
HIGHEST = lax.Precision.HIGHEST


def frequencies(channels):
    return 1.0 + 0.5 * jnp.arange(channels, dtype=jnp.float32) / channels


def basis_table(channels):
    centre = (jnp.arange(channels, dtype=jnp.float32) - 0.5 * (channels - 1)) / channels
    columns = [jnp.ones_like(centre), centre, centre * centre]
    finished = []
    for column in columns:
        for before in finished:
            column = column - jnp.sum(column * before) * before
        finished.append(column / jnp.sqrt(jnp.sum(column * column)))
    return jnp.stack(finished, axis=1)


def group_sources(source_lmn, source_flux, cluster_map, directions):
    ranking = jnp.argsort(cluster_map, stable=True)
    cosines = jnp.take(source_lmn, ranking, axis=1).reshape(3, directions, -1)
    brightness = jnp.take(source_flux, ranking).reshape(directions, -1)
    return (jnp.moveaxis(cosines, 1, 0), brightness)


def contract(row_part, column_part):
    return jnp.einsum("ctps,ctjs->cjtp", row_part, column_part, precision=HIGHEST)


def model_block(positions, direction_cosines, weights, freq_scale, column_ids):
    projected = (
        positions[0][:, :, None] * direction_cosines[0]
        + positions[1][:, :, None] * direction_cosines[1]
    )
    projected = projected + positions[2][:, :, None] * direction_cosines[2]
    phases = 2.0 * math.pi * freq_scale[:, None, None, None] * projected[None]
    cosine = jnp.cos(phases)
    sine_part = jnp.sin(phases)
    weighted_cos = cosine * weights
    weighted_sin = sine_part * weights
    column_cos = jnp.take(cosine, column_ids, axis=2)
    column_sin = jnp.take(sine_part, column_ids, axis=2)
    model_real = contract(weighted_cos, column_cos) + contract(weighted_sin, column_sin)
    model_imag = contract(weighted_sin, column_cos) - contract(weighted_cos, column_sin)
    station_ids = jnp.arange(positions.shape[2], dtype=jnp.int32)
    retained = (column_ids[:, None] != station_ids[None, :]).astype(model_real.dtype)
    retained = retained[None, :, None, :]
    return (model_real * retained, model_imag * retained)


def build_models(positions, cosines, brightness, freq_scale, column_ids):

    def one_model(entry):
        return model_block(positions, entry[0], entry[1], freq_scale, column_ids)

    return lax.map(one_model, (cosines, brightness))


def gain_update(numerator, denominator, gains, consensus, multiplier, penalty):
    weight_pen = penalty[:, None]
    scaling = 1.0 / (denominator + weight_pen)
    fresh = (numerator + gains * denominator + weight_pen * (consensus - multiplier)) * scaling
    return 0.5 * (gains + fresh)


def pass_terms(visibilities, gains, model_real, model_imag, column_ids):
    column_gains = jnp.take(gains, column_ids, axis=3)
    column_real = jnp.moveaxis(column_gains[0], 1, 0)[:, :, :, None, None]
    column_imag = jnp.moveaxis(column_gains[1], 1, 0)[:, :, :, None, None]
    row_real = jnp.moveaxis(gains[0], 1, 0)[:, :, None, None, :]
    row_imag = jnp.moveaxis(gains[1], 1, 0)[:, :, None, None, :]
    along_real = model_real * column_real + model_imag * column_imag
    along_imag = model_imag * column_real - model_real * column_imag
    pred_real = row_real * along_real - row_imag * along_imag
    pred_imag = row_real * along_imag + row_imag * along_real
    resid_real = visibilities[0] - jnp.sum(pred_real, axis=0)
    resid_imag = visibilities[1] - jnp.sum(pred_imag, axis=0)
    num_real = jnp.sum(resid_real * along_real + resid_imag * along_imag, axis=(2, 3))
    num_imag = jnp.sum(resid_imag * along_real - resid_real * along_imag, axis=(2, 3))
    denominator = jnp.sum(along_real * along_real + along_imag * along_imag, axis=(2, 3))
    numerator = jnp.moveaxis(jnp.stack([num_real, num_imag]), 1, 2)
    return (numerator, jnp.moveaxis(denominator, 0, 1)[None])


def channel_fit(values, local_basis):
    partial_sums = jnp.einsum("fj,rfkp->rjkp", local_basis, values, precision=HIGHEST)
    coefficients = lax.psum(partial_sums, "freq")
    return jnp.einsum("fj,rjkp->rfkp", local_basis, coefficients, precision=HIGHEST)


def on_device(
    visibilities, positions, source_lmn, source_flux, cluster_map, station_order, penalty, offsets
):
    chan_dev = visibilities.shape[1]
    column_count = visibilities.shape[2]
    stations = visibilities.shape[4]
    directions = penalty.shape[0]
    channels = chan_dev * lax.axis_size("freq")
    row_index = lax.axis_index("freq")
    col_index = lax.axis_index("stcol")
    owned_count = stations // lax.axis_size("stcol")
    column_ids = lax.dynamic_slice_in_dim(station_order, col_index * column_count, column_count)
    freq_scale = lax.dynamic_slice_in_dim(frequencies(channels), row_index * chan_dev, chan_dev)
    basis = basis_table(channels)
    local_basis = lax.dynamic_slice_in_dim(basis, row_index * chan_dev, chan_dev, 0)
    cosines, brightness = group_sources(source_lmn, source_flux, cluster_map, directions)
    model_real, model_imag = build_models(positions, cosines, brightness, freq_scale, column_ids)
    gains = jnp.stack([1.0 + offsets[0], offsets[1]])
    consensus = gains
    multiplier = jnp.zeros_like(gains)
    for admm_step in range(ADMM):
        for sweep_index in range(PASSES):
            numerator, denominator = pass_terms(
                visibilities, gains, model_real, model_imag, column_ids
            )
            numerator, denominator = lax.psum((numerator, denominator), "stcol")
            gains = gain_update(numerator, denominator, gains, consensus, multiplier, penalty)
        consensus = channel_fit(gains + multiplier, local_basis)
        multiplier = multiplier + gains - consensus
    gains_out = lax.dynamic_slice_in_dim(gains, col_index * owned_count, owned_count, 3)
    cons_out = lax.dynamic_slice_in_dim(consensus, col_index * owned_count, owned_count, 3)
    return (gains_out, cons_out)


def solution(mesh):
    in_specs = (
        P(None, "freq", "stcol", None, None),
        P(),
        P(),
        P(),
        P(),
        P(),
        P(),
        P(None, "freq", None, None),
    )
    out_specs = (P(None, "freq", None, "stcol"), P(None, "freq", None, "stcol"))
    return jax.shard_map(
        on_device, mesh=mesh, in_specs=in_specs, out_specs=out_specs, check_vma=False
    )
```

profile of v0, /device:TPU:0, one launch (start us, length us, event | category | flops | bytes accessed | tf_op | source)
XLA Modules:
  0.0 582.2 jit_solution(7560727911189916129)
XLA Ops:
  7.3 5.1 sort.17
  16.7 2.8 gather_fusion.2
  19.9 4.5 gather_fusion.3
  25.8 137.8 %while.14 = (s32[]{:T(128)}, f32[16,1,64,1,512]{4,2,3,1,0:T(8,128)S(1)}, f32[16,1,64,1,512]{4,2,3,1,0:T(8,128)}, s32[64]{0:T(128)S(1)}, f32[1,1,1,1]{3,2,1,0:T(1...) while((s32[]{:T(128)}, ...), condition=%wide.region_2.4_spmd, body=%wide.region_1.3_spmd.sunk | while | flops 101992000 | bytes 1256825 | solution.py:64
  29.5 2.0 fusion.98
  33.0 1.4 fusion.96
  38.1 2.1 fusion.98
  41.6 1.4 fusion.96
  46.7 2.1 fusion.98
  50.2 1.4 fusion.96
  55.4 2.1 fusion.98
  64.0 2.1 fusion.98
  72.6 2.0 fusion.98
  76.0 1.4 fusion.96
  81.2 2.1 fusion.98
  89.8 2.1 fusion.98
  93.3 1.4 fusion.96
  98.4 2.0 fusion.98
  101.9 1.4 fusion.96
  107.0 2.1 fusion.98
  110.5 1.4 fusion.96
  115.7 2.0 fusion.98
  119.1 1.4 fusion.96
  124.3 2.1 fusion.98
  127.7 1.4 fusion.96
  132.9 2.0 fusion.98
  141.5 2.1 fusion.98
  144.9 1.4 fusion.96
  150.1 2.0 fusion.98
  153.5 1.4 fusion.96
  158.7 2.1 fusion.98
  162.2 1.4 fusion.96
  163.6 2.6 subtract_reduce_fusion.7
  169.5 38.9 %psum.71 = f32[1,1,16,512]{3,2,1,0:T(8,128)S(1)} all-reduce(f32[1,1,16,512]{3,2,1,0:T(8,128)S(1)} %bitcast.261), channel_id=1, replica_groups=mesh['freq'=4,'stcol'=8] {'stcol'}, use_global_device_ids=true, to_apply=%region_9.12 | all-reduce | flops 8192 | bytes 65536 | tf_op jit(solution)/shard_map/psum | solution.py:124
  214.6 25.7 %all-reduce.7.cloned.1.call-done = f32[2,1,16,512]{3,2,1,0:T(8,128)} async-done(((f32[2,1,16,512]{3,2,1,0:T(8,128)}), f32[2,1,16,512]{3,2,1,0:T(8,128)}) %all-reduce.7.cloned.1.call-update) | async-done | bytes 65552 | tf_op jit(solution)/shard_map/psum | solution.py:124
  243.5 2.6 subtract_reduce_fusion.5
  248.1 36.2 %psum.73 = f32[1,1,16,512]{3,2,1,0:T(8,128)S(1)} all-reduce(f32[1,1,16,512]{3,2,1,0:T(8,128)S(1)} %bitcast.262), channel_id=1, replica_groups=mesh['freq'=4,'stcol'=8] {'stcol'}, use_global_device_ids=true, to_apply=%region_16.19 | all-reduce | flops 8192 | bytes 65536 | tf_op jit(solution)/shard_map/psum | solution.py:124
  284.4 33.1 %all-reduce.9.cloned.1.call-done = f32[2,1,16,512]{3,2,1,0:T(8,128)} async-done(((f32[2,1,16,512]{3,2,1,0:T(8,128)}), f32[2,1,16,512]{3,2,1,0:T(8,128)}) %all-reduce.9.cloned.1.call-update) | async-done | bytes 65552 | tf_op jit(solution)/shard_map/psum | solution.py:124
  319.8 2.6 subtract_reduce_fusion.3
  323.7 36.1 %psum.75 = f32[1,1,16,512]{3,2,1,0:T(8,128)S(1)} all-reduce(f32[1,1,16,512]{3,2,1,0:T(8,128)S(1)} %bitcast.264), channel_id=1, replica_groups=mesh['freq'=4,'stcol'=8] {'stcol'}, use_global_device_ids=true, to_apply=%region_23.26 | all-reduce | flops 8192 | bytes 65536 | tf_op jit(solution)/shard_map/psum | solution.py:124
  361.4 28.7 %all-reduce.13.cloned.1.call-done = f32[2,3,16,512]{3,2,1,0:T(8,128)} async-done(((f32[2,3,16,512]{3,2,1,0:T(8,128)}), f32[2,3,16,512]{3,2,1,0:T(8,128)}) %all-reduce.13.cloned.1.call-update) | async-done | bytes 196624 | tf_op jit(solution)/shard_map/psum | solution.py:95
  390.1 1.6 fusion.59
  391.7 71.0 %all-reduce.11.cloned.1.call-done = f32[2,1,16,512]{3,2,1,0:T(8,128)} async-done(((f32[2,1,16,512]{3,2,1,0:T(8,128)}), f32[2,1,16,512]{3,2,1,0:T(8,128)}) %all-reduce.11.cloned.1.call-update) | async-done | bytes 65552 | tf_op jit(solution)/shard_map/psum | solution.py:124
  465.0 2.6 subtract_reduce_fusion.1
  469.5 36.2 %psum.78 = f32[1,1,16,512]{3,2,1,0:T(8,128)S(1)} all-reduce(f32[1,1,16,512]{3,2,1,0:T(8,128)S(1)} %bitcast.263), channel_id=1, replica_groups=mesh['freq'=4,'stcol'=8] {'stcol'}, use_global_device_ids=true, to_apply=%region_36.39 | all-reduce | flops 8192 | bytes 65536 | tf_op jit(solution)/shard_map/psum | solution.py:124
  505.8 33.1 %all-reduce.15.cloned.1.call-done = f32[2,1,16,512]{3,2,1,0:T(8,128)} async-done(((f32[2,1,16,512]{3,2,1,0:T(8,128)}), f32[2,1,16,512]{3,2,1,0:T(8,128)}) %all-reduce.15.cloned.1.call-update) | async-done | bytes 65552 | tf_op jit(solution)/shard_map/psum | solution.py:124
  541.3 31.8 %all-reduce.17.cloned.1.call-done = f32[2,3,16,512]{3,2,1,0:T(8,128)} async-done(((f32[2,3,16,512]{3,2,1,0:T(8,128)}), f32[2,3,16,512]{3,2,1,0:T(8,128)}) %all-reduce.17.cloned.1.call-update) | async-done | bytes 196624 | tf_op jit(solution)/shard_map/psum | solution.py:95
  573.1 1.6 fusion.57
  (315 shorter events, 116.7 us)
Async XLA Ops:
  7.2 12.7 %copy-start = (f32[1024]{0:T(1024)S(1)}, f32[1024]{0:T(1024)}, u32[]{:S(2)}) copy-start(f32[1024]{0:T(1024)} %param.17) | copy-start | bytes 12292
  7.2 233.1 %all-reduce.7.cloned.1.call-start = ((), (), s32[]{:S(2)}) async-start(), calls=%async_computation | async-start | bytes 131072 | tf_op jit(solution)/shard_map/psum | solution.py:124
  13.1 0.8 copy-start.7
  13.1 1.9 copy-start.6
  19.9 5.9 %copy-start.3 = (f32[3,1,512]{2,1,0:T(1,128)S(1)}, f32[3,1,512]{2,1,0:T(1,128)}, u32[]{:S(2)}) copy-start(f32[3,1,512]{2,1,0:T(1,128)} %param.15) | copy-start | bytes 18436
  19.9 5.9 %copy-start.8 = (s32[64]{0:T(128)S(1)}, s32[64]{0:T(128)}, u32[]{:S(2)}) copy-start(s32[64]{0:T(128)} %copy-done.7) | copy-start | bytes 772
  25.8 137.8 %copy-start.5 = (f32[16,64]{1,0:T(8,128)S(1)}, f32[16,64]{1,0:T(8,128)}, u32[]{:S(2)}) copy-start(f32[16,64]{1,0:T(8,128)} %copy.125) | copy-start | bytes 12292
  163.6 2.6 copy-start.1
  166.5 47.9 %copy-start.4 = (f32[16]{0:T(128)S(1)}, f32[16]{0:T(128)}, u32[]{:S(2)}) copy-start(f32[16]{0:T(128)} %param.20) | copy-start | bytes 196
  168.2 149.4 %all-reduce.9.cloned.1.call-start = ((), (), s32[]{:S(2)}) async-start(), calls=%async_computation.1 | async-start | bytes 131072 | tf_op jit(solution)/shard_map/psum | solution.py:124
  246.4 71.1 %copy-start.2 = (f32[2,1,16,512]{3,2,1,0:T(8,128)S(1)}, f32[2,1,16,512]{3,2,1,0:T(8,128)}, u32[]{:S(2)}) copy-start(f32[2,1,16,512]{3,2,1,0:T(8,128)} %all-reduce.7.cloned.1.call-done) | copy-start | bytes 196612
  248.1 142.0 %all-reduce.13.cloned.1.call-start = ((), (), s32[]{:S(2)}) async-start(), calls=%async_computation.3 | async-start | bytes 393216 | tf_op jit(solution)/shard_map/psum | solution.py:95
  360.7 102.0 %all-reduce.11.cloned.1.call-start = ((), (), s32[]{:S(2)}) async-start(), calls=%async_computation.2 | async-start | bytes 131072 | tf_op jit(solution)/shard_map/psum | solution.py:124
  361.4 177.5 %all-reduce.15.cloned.1.call-start = ((), (), s32[]{:S(2)}) async-start(), calls=%async_computation.4 | async-start | bytes 131072 | tf_op jit(solution)/shard_map/psum | solution.py:124
  469.5 103.6 %all-reduce.17.cloned.1.call-start = ((), (), s32[]{:S(2)}) async-start(), calls=%async_computation.5 | async-start | bytes 393216 | tf_op jit(solution)/shard_map/psum | solution.py:95
Sparse Core Ops, SparseCore 0:
  168.3 71.9 all-reduce.6
  248.2 69.2 all-reduce.8
  360.8 29.2 all-reduce.12
  393.4 69.2 all-reduce.10
  469.6 69.2 all-reduce.14
  541.1 31.9 all-reduce.16
where the time goes:
time: 583 us; the launch traced here: 582 us
  waiting for transfers between devices  223 us (38%)
  blocking collectives  147 us (25%)
  matrix products  103 us (18%)
  other arithmetic  52.9 us (9%)
  local copies, waits for them, and re-layouts  35.6 us (6%)
  between operations  18 us (3%)
    psum x4, waiting for transfers between devices, on_device(): numerator, denominator = lax.psum((numerator, denominator), 'stcol')  163 us
    psum x4, blocking collectives, on_device(): numerator, denominator = lax.psum((numerator, denominator), 'stcol')  147 us
    dot_general x64, matrix products, contract(): jnp.einsum('ctps,ctjs->cjtp', row_part, column_part, precision=HIGHEST)  100 us
    psum x2, waiting for transfers between devices, channel_fit(): coefficients = lax.psum(partial_sums, 'freq')  60.4 us
    another operation x16, other arithmetic, model_block(): column_sin = jnp.take(sine_part, column_ids, axis=2)  16.5 us
  transfers between devices with their start and end apart: 6, of which 6 were waited for; matrix products, arithmetic and copies ran while one was open for 1% of the time, Pallas kernels for 0%

commit v1 on v0

--- a/solution.py
+++ b/solution.py
@@ -92,7 +92,7 @@
 
 def channel_fit(values, local_basis):
     partial_sums = jnp.einsum("fj,rfkp->rjkp", local_basis, values, precision=HIGHEST)
-    coefficients = lax.psum(partial_sums, "freq")
+    coefficients = jnp.sum(lax.all_gather(partial_sums, "freq"), axis=0)
     return jnp.einsum("fj,rjkp->rfkp", local_basis, coefficients, precision=HIGHEST)
 
 

time: 583 us -> 488 us (0.84)
  waiting for transfers between devices: 223 us -> 116 us
  blocking collectives: 147 us -> 165 us
    psum x2 -> x0, waiting for transfers between devices: 60.4 us -> none  [channel_fit(): coefficients = lax.psum(partial_sums, 'freq')]
    psum x4, waiting for transfers between devices: 163 us -> 116 us  [on_device(): numerator, denominator = lax.psum((numerator, denominator), 'stcol')]
    all_gather x0 -> x2, blocking collectives: none -> 17.1 us  [channel_fit(): coefficients = jnp.sum(lax.all_gather(partial_sums, 'freq'), axis=0)]
  transfers between devices with their start and end apart: 6 -> 4, of which waited for: 6 -> 4; matrix products, arithmetic and copies ran while one was open for 1% -> 1% of each run, Pallas kernels for 0% -> 0%
where the time goes in v1:
time: 488 us; the launch traced here: 487 us
  blocking collectives  165 us (34%)
  waiting for transfers between devices  116 us (24%)
  matrix products  102 us (21%)
  other arithmetic  51.4 us (11%)
  local copies, waits for them, and re-layouts  34.6 us (7%)
  between operations  17.6 us (4%)
    psum x4, blocking collectives, on_device(): numerator, denominator = lax.psum((numerator, denominator), 'stcol')  147 us
    psum x4, waiting for transfers between devices, on_device(): numerator, denominator = lax.psum((numerator, denominator), 'stcol')  116 us
    dot_general x64, matrix products, contract(): jnp.einsum('ctps,ctjs->cjtp', row_part, column_part, precision=HIGHEST)  100 us
    all_gather x2, blocking collectives, channel_fit(): coefficients = jnp.sum(lax.all_gather(partial_sums, 'freq'), axis=0)  17.1 us
    another operation x16, other arithmetic, model_block(): column_sin = jnp.take(sine_part, column_ids, axis=2)  16.5 us
    reduce_sum x4, other arithmetic, pass_terms(): resid_real = visibilities[0] - jnp.sum(pred_real, axis=0)  10.2 us
  transfers between devices with their start and end apart: 4, of which 4 were waited for; matrix products, arithmetic and copies ran while one was open for 1% of the time, Pallas kernels for 0%

profile of v1, /device:TPU:0, one launch (start us, length us, event | category | flops | bytes accessed | tf_op | source)
XLA Modules:
  0.0 487.1 jit_solution(12452180796771630538)
XLA Ops:
  7.3 5.1 %sort.17 = (s32[1024]{0:T(1024)}, s32[1024]{0:T(1024)S(1)}) sort(s32[1024]{0:T(1024)} %param.18, s32[1024]{0:T(1024)S(1)} %iota.29), dimensions={0}, to_apply=%region_0.0 | sort | flops 10240 | bytes 16384 | tf_op jit(solution)/shard_map/jit(argsort)/sort | solution.py:28
  16.1 2.8 gather_fusion.2
  19.2 4.5 gather_fusion.3
  25.1 137.8 %while.14 = (s32[]{:T(128)}, f32[16,1,64,1,512]{4,2,3,1,0:T(8,128)S(1)}, f32[16,1,64,1,512]{4,2,3,1,0:T(8,128)}, s32[64]{0:T(128)S(1)}, f32[1,1,1,1]{3,2,1,0:T(1...) while((s32[]{:T(128)}, ...), condition=%wide.region_2.4_spmd, body=%wide.region_1.3_spmd.sunk | while | flops 101992000 | bytes 1256825 | solution.py:64
  28.9 2.0 fusion.98
  32.3 1.4 fusion.96
  37.5 2.1 fusion.98
  40.9 1.4 fusion.96
  46.1 2.1 fusion.98
  49.6 1.4 fusion.96
  54.7 2.1 fusion.98
  58.2 1.4 fusion.96
  63.3 2.1 fusion.98
  72.0 2.0 fusion.98
  75.4 1.4 fusion.96
  80.6 2.1 fusion.98
  84.0 1.4 fusion.96
  89.2 2.1 fusion.98
  92.6 1.4 fusion.96
  97.8 2.0 fusion.98
  101.2 1.4 fusion.96
  106.4 2.1 fusion.98
  109.9 1.4 fusion.96
  115.0 2.0 fusion.98
  118.5 1.4 fusion.96
  123.6 2.1 fusion.98
  127.1 1.4 fusion.96
  132.2 2.0 fusion.98
  140.9 2.1 fusion.98
  144.3 1.4 fusion.96
  149.5 2.0 fusion.98
  152.9 1.4 fusion.96
  158.1 2.1 fusion.98
  161.5 1.4 fusion.96
  163.0 2.6 subtract_reduce_fusion.7
  168.8 38.9 %psum.57 = f32[1,1,16,512]{3,2,1,0:T(8,128)S(1)} all-reduce(f32[1,1,16,512]{3,2,1,0:T(8,128)S(1)} %bitcast.265), channel_id=1, replica_groups=mesh['freq'=4,'stcol'=8] {'stcol'}, use_global_device_ids=true, to_apply=%region_9.12 | all-reduce | flops 8192 | bytes 65536 | tf_op jit(solution)/shard_map/psum | solution.py:124
  213.7 26.0 %all-reduce.5.cloned.1.call-done = f32[2,1,16,512]{3,2,1,0:T(8,128)} async-done(((f32[2,1,16,512]{3,2,1,0:T(8,128)}), f32[2,1,16,512]{3,2,1,0:T(8,128)}) %all-reduce.5.cloned.1.call-update) | async-done | bytes 65552 | tf_op jit(solution)/shard_map/psum | solution.py:124
  242.8 2.5 subtract_reduce_fusion.5
  247.3 36.2 %psum.59 = f32[1,1,16,512]{3,2,1,0:T(8,128)S(1)} all-reduce(f32[1,1,16,512]{3,2,1,0:T(8,128)S(1)} %bitcast.266), channel_id=1, replica_groups=mesh['freq'=4,'stcol'=8] {'stcol'}, use_global_device_ids=true, to_apply=%region_16.19 | all-reduce | flops 8192 | bytes 65536 | tf_op jit(solution)/shard_map/psum | solution.py:124
  283.6 33.1 %all-reduce.7.cloned.1.call-done = f32[2,1,16,512]{3,2,1,0:T(8,128)} async-done(((f32[2,1,16,512]{3,2,1,0:T(8,128)}), f32[2,1,16,512]{3,2,1,0:T(8,128)}) %all-reduce.7.cloned.1.call-update) | async-done | bytes 65552 | tf_op jit(solution)/shard_map/psum | solution.py:124
  318.9 2.5 subtract_reduce_fusion.3
  323.5 36.2 %psum.61 = f32[1,1,16,512]{3,2,1,0:T(8,128)S(1)} all-reduce(f32[1,1,16,512]{3,2,1,0:T(8,128)S(1)} %bitcast.267), channel_id=1, replica_groups=mesh['freq'=4,'stcol'=8] {'stcol'}, use_global_device_ids=true, to_apply=%region_23.26 | all-reduce | flops 8192 | bytes 65536 | tf_op jit(solution)/shard_map/psum | solution.py:124
  359.7 8.6 %all-gather = f32[8,3,16,512]{3,2,1,0:T(8,128)S(1)} all-gather(f32[2,3,16,512]{3,2,1,0:T(8,128)S(1)} %multiply_bitcast_fusion.1), channel_id=2, replica_groups=mesh['freq'=4,'stcol'=8] {'freq'}, dimensions={0}, use_global_device_ids=true | all-gather | bytes 983040 | tf_op jit(solution)/shard_map/all_gather | solution.py:95
  369.1 23.8 %all-reduce.9.cloned.1.call-done = f32[2,1,16,512]{3,2,1,0:T(8,128)} async-done(((f32[2,1,16,512]{3,2,1,0:T(8,128)}), f32[2,1,16,512]{3,2,1,0:T(8,128)}) %all-reduce.9.cloned.1.call-update) | async-done | bytes 65552 | tf_op jit(solution)/shard_map/psum | solution.py:124
  395.0 2.5 subtract_reduce_fusion.1
  399.5 36.2 %psum.63 = f32[1,1,16,512]{3,2,1,0:T(8,128)S(1)} all-reduce(f32[1,1,16,512]{3,2,1,0:T(8,128)S(1)} %bitcast.268), channel_id=1, replica_groups=mesh['freq'=4,'stcol'=8] {'stcol'}, use_global_device_ids=true, to_apply=%region_36.39 | all-reduce | flops 8192 | bytes 65536 | tf_op jit(solution)/shard_map/psum | solution.py:124
  435.8 33.1 %all-reduce.11.cloned.1.call-done = f32[2,1,16,512]{3,2,1,0:T(8,128)} async-done(((f32[2,1,16,512]{3,2,1,0:T(8,128)}), f32[2,1,16,512]{3,2,1,0:T(8,128)}) %all-reduce.11.cloned.1.call-update) | async-done | bytes 65552 | tf_op jit(solution)/shard_map/psum | solution.py:124
  469.9 8.6 %all-gather.1 = f32[8,3,16,512]{3,2,1,0:T(8,128)S(1)} all-gather(f32[2,3,16,512]{3,2,1,0:T(8,128)S(1)} %multiply_bitcast_fusion), channel_id=3, replica_groups=mesh['freq'=4,'stcol'=8] {'freq'}, dimensions={0}, use_global_device_ids=true | all-gather | bytes 983040 | tf_op jit(solution)/shard_map/all_gather | solution.py:95
  (305 shorter events, 112.6 us)
Async XLA Ops:
  7.2 12.1 %copy-start = (f32[1024]{0:T(1024)S(1)}, f32[1024]{0:T(1024)}, u32[]{:S(2)}) copy-start(f32[1024]{0:T(1024)} %param.17) | copy-start | bytes 12292
  7.2 232.5 %all-reduce.5.cloned.1.call-start = ((), (), s32[]{:S(2)}) async-start(), calls=%async_computation | async-start | bytes 131072 | tf_op jit(solution)/shard_map/psum | solution.py:124
  19.2 5.9 %copy-start.3 = (f32[3,1,512]{2,1,0:T(1,128)S(1)}, f32[3,1,512]{2,1,0:T(1,128)}, u32[]{:S(2)}) copy-start(f32[3,1,512]{2,1,0:T(1,128)} %param.15) | copy-start | bytes 18436
  162.9 2.6 copy-start.1
  165.9 47.6 %copy-start.4 = (f32[16]{0:T(128)S(1)}, f32[16]{0:T(128)}, u32[]{:S(2)}) copy-start(f32[16]{0:T(128)} %param.20) | copy-start | bytes 196
  167.5 149.2 %all-reduce.7.cloned.1.call-start = ((), (), s32[]{:S(2)}) async-start(), calls=%async_computation.1 | async-start | bytes 131072 | tf_op jit(solution)/shard_map/psum | solution.py:124
  245.6 71.1 %copy-start.2 = (f32[2,1,16,512]{3,2,1,0:T(8,128)S(1)}, f32[2,1,16,512]{3,2,1,0:T(8,128)}, u32[]{:S(2)}) copy-start(f32[2,1,16,512]{3,2,1,0:T(8,128)} %all-reduce.5.cloned.1.call-done) | copy-start | bytes 196612
  247.3 145.6 %all-reduce.9.cloned.1.call-start = ((), (), s32[]{:S(2)}) async-start(), calls=%async_computation.2 | async-start | bytes 131072 | tf_op jit(solution)/shard_map/psum | solution.py:124
  323.4 145.5 %all-reduce.11.cloned.1.call-start = ((), (), s32[]{:S(2)}) async-start(), calls=%async_computation.3 | async-start | bytes 131072 | tf_op jit(solution)/shard_map/psum | solution.py:124
Sparse Core Ops, SparseCore 0:
  167.6 71.9 all-reduce.4
  247.4 69.2 all-reduce.6
  323.5 69.2 all-reduce.8
  399.6 69.2 all-reduce.10
